TPU v7x, 512 devices: a whole 4x8x8 slice. The times are simulated.
512 devices in a mesh: dev: 32 (over y_hi, z), ha: 2 (over y_lo), col: 8 (over x, core).
Axes of the slice: x: 4, y: 8 (y_hi: 4, y_lo: 2; y = y_hi * 2 + y_lo), z: 8, core: 2. Of those that a mesh axis runs over, the one named last changes fastest.
Arguments:
- features: bfloat16 [128, 128, 32, 128], P('col', 'dev', 'ha'), may hold values from -6 to 6
- kernel: bfloat16 [3, 3, 3, 128, 128], P(None, None, None, 'col'), may hold values from -0.109375 to 0.109375
- channel_bias: float32 [128], P('col'), may hold values from -3 to 3
Outputs:
- activated: bfloat16 [128, 128, 32, 128], P('col', 'dev', 'ha')
All inputs are finite; a program needn't handle non-finite values.
Results may differ from a plain program's by a relative error of at most 0.005.
Values may be sent and summed in bfloat16 or wider, within the bound.
A program may use at most 64 MiB of HBM per device.

v0:
```python
import jax
import jax.numpy as jnp
from jax import lax
from jax.sharding import PartitionSpec as P


def with_halo(x, sides, width):
    for axis, dim in sides:
        devices, length = (lax.axis_size(axis), x.shape[dim])
        up = [(i, (i + 1) % devices) for i in range(devices - 1)]
        down = [(j, i) for i, j in up]
        last = lax.slice_in_dim(x, length - width, length, axis=dim)
        first = lax.slice_in_dim(x, 0, width, axis=dim)
        before = lax.ppermute(last, axis, up)
        after = lax.ppermute(first, axis, down)
        x = jnp.concatenate([before, x, after], axis=dim)
    return x


def convolve(padded, weights):
    depth_pad = padded.shape[1]
    height_pad = padded.shape[2]
    width_cells = padded.shape[3]
    outer = weights.shape[3]
    depth_cells = depth_pad - 2
    height_cells = height_pad - 2
    partial_sums = [
        jnp.zeros((outer, depth_cells, height_cells, width_cells), jnp.float32)
        for col_tap in range(3)
    ]
    for depth_tap in range(3):
        planes = padded[:, depth_tap : depth_tap + depth_cells]
        tap_out = lax.dot_general(
            weights[depth_tap], planes, (((3,), (0,)), ((), ())), preferred_element_type=jnp.float32
        )
        for row_tap in range(3):
            for col_tap in range(3):
                partial_sums[col_tap] = (
                    partial_sums[col_tap]
                    + tap_out[row_tap, col_tap, :, :, row_tap : row_tap + height_cells, :]
                )
    zero_column = jnp.zeros((outer, depth_cells, height_cells, 1), jnp.float32)
    from_left = jnp.concatenate([zero_column, partial_sums[0][..., :-1]], axis=3)
    from_right = jnp.concatenate([partial_sums[2][..., 1:], zero_column], axis=3)
    return partial_sums[1] + from_left + from_right


def finish(summed, offsets):
    summed = summed + offsets[:, None, None, None]
    return jnp.where(summed >= 0, summed, 0.3 * summed).astype(jnp.bfloat16)


def per_device(features, kernel, channel_bias):
    padded = with_halo(features, (("dev", 1), ("ha", 2)), 1)
    gathered = lax.all_gather(padded, "col", axis=0, tiled=True)
    return finish(convolve(gathered, kernel), channel_bias)


def solution(mesh):
    in_specs = (P("col", "dev", "ha", None), P(None, None, None, "col", None), P("col"))
    out_specs = P("col", "dev", "ha", None)
    return jax.shard_map(
        per_device, mesh=mesh, in_specs=in_specs, out_specs=out_specs, check_vma=False
    )
```

profile of v0, /device:TPU:1, one launch (start us, length us, event | category | flops | bytes accessed | tf_op | source)
XLA Modules:
  0.0 85.2 jit_solution(9481461446292273636)
XLA Ops:
  6.5 0.0 all-gather.2.cloned.1.call-start
  6.5 0.9 %fusion.24 = (bf16[16,1,16,128]{3,2,1,0:T(8,128)(2,1)S(1)}, bf16[16,1,16,128]{3,2,1,0:T(8,128)(2,1)S(1)}) fusion(bf16[16,4,16,128]{3,2,1,0:T(8,128)(2,1)} %param.3), kind=kLoop, calls=%fused_computation.61 | loop fusion | bytes 262144 | tf_op jit(solution)/shard_map/slice | solution.py:13
  7.5 4.8 %collective-permute-start = (bf16[16,1,16,128]{3,0,2,1:T(8,128)(2,1)S(1)}, bf16[16,1,16,128]{3,0,2,1:T(8,128)(2,1)S(1)}, u32[]{:S(2)}, u32[]{:S(2)}) collective-permute-start(bf16[16,1,16,128]{3,0,2,1:T(8,128)(2,1)S(1)} %copy.37), channel_id=1, source_target_pairs={{0,16},{16,32},{32,48},{48,64},{64,80},{80,96},{96,112},{112,128},... | collective-permute-start | bytes 196616 | tf_op jit(solution)/shard_map/ppermute | solution.py:14
  12.3 1.3 %collective-permute-start.1 = (bf16[16,1,16,128]{3,0,2,1:T(8,128)(2,1)S(1)}, bf16[16,1,16,128]{3,0,2,1:T(8,128)(2,1)S(1)}, u32[]{:S(2)}, u32[]{:S(2)}) collective-permute-start(bf16[16,1,16,128]{3,0,2,1:T(8,128)(2,1)S(1)} %copy.38), channel_id=1, source_target_pairs={{16,0},{32,16},{48,32},{64,48},{80,64},{96,80},{112,96},{128,112},... | collective-permute-start | bytes 196616 | tf_op jit(solution)/shard_map/ppermute | solution.py:15
  13.6 0.0 collective-permute-done
  13.6 1.1 %constant_dynamic-update-slice_fusion.1 = bf16[16,6,16,128]{3,0,2,1:T(8,128)(2,1)S(1)} fusion(bf16[16,6,16,128]{3,0,2,1:T(8,128)(2,1)S(1)} %constant_dynamic-update-slice_fusion.2, bf16[16,4,16,128]{3,2,1,0:T(8,128)(2,1)} %param.3), kind=kLoop, calls=%fused_computation.58 | loop fusion | bytes 524288
  14.8 3.2 %collective-permute-done.1 = bf16[16,1,16,128]{3,0,2,1:T(8,128)(2,1)S(1)} collective-permute-done((bf16[16,1,16,128]{3,0,2,1:T(8,128)(2,1)S(1)}, bf16[16,1,16,128]{3,0,2,1:T(8,128)(2,1)S(1)}, u32[]{:S(2)}, u32[]{:S(2)}) %collective-permute-start.1) | collective-permute-done | bytes 65568 | tf_op jit(solution)/shard_map/ppermute | solution.py:15
  18.0 3.2 %collective-permute-start.2 = (bf16[16,6,1,128]{3,0,2,1:T(8,128)(2,1)S(1)}, bf16[16,6,1,128]{3,0,2,1:T(8,128)(2,1)S(1)}, u32[]{:S(2)}, u32[]{:S(2)}) collective-permute-start(bf16[16,6,1,128]{3,0,2,1:T(8,128)(2,1)S(1)} %get-tuple-element.5), channel_id=1, source_target_pairs={{0,8},{1,9},{2,10},{3,11},{4,12},{5,13},{6,14},{7,15},{16,24},{17,... | collective-permute-start | bytes 73736 | tf_op jit(solution)/shard_map/ppermute | solution.py:14
  21.2 1.3 %collective-permute-start.3 = (bf16[16,6,1,128]{3,0,2,1:T(8,128)(2,1)S(1)}, bf16[16,6,1,128]{3,0,2,1:T(8,128)(2,1)S(1)}, u32[]{:S(2)}, u32[]{:S(2)}) collective-permute-start(bf16[16,6,1,128]{3,0,2,1:T(8,128)(2,1)S(1)} %get-tuple-element.6), channel_id=1, source_target_pairs={{8,0},{9,1},{10,2},{11,3},{12,4},{13,5},{14,6},{15,7},{24,16},{25,... | collective-permute-start | bytes 73736 | tf_op jit(solution)/shard_map/ppermute | solution.py:15
  22.5 0.0 collective-permute-done.2
  22.5 3.3 %collective-permute-done.3 = bf16[16,6,1,128]{3,0,2,1:T(8,128)(2,1)S(1)} collective-permute-done((bf16[16,6,1,128]{3,0,2,1:T(8,128)(2,1)S(1)}, bf16[16,6,1,128]{3,0,2,1:T(8,128)(2,1)S(1)}, u32[]{:S(2)}, u32[]{:S(2)}) %collective-permute-start.3) | collective-permute-done | bytes 24608 | tf_op jit(solution)/shard_map/ppermute | solution.py:15
  25.8 0.8 pad_maximum_fusion
  26.6 0.0 all-gather.2.cloned.1.call-update
  26.7 0.0 copy-start.1
  26.7 45.2 %all-gather.2.cloned.1.call-done = bf16[128,6,18,128]{3,0,2,1:T(8,128)(2,1)} async-done(((bf16[16,6,18,128]{3,0,2,1:T(8,128)(2,1)}), bf16[128,6,18,128]{3,0,2,1:T(8,128)(2,1)}) %all-gather.2.cloned.1.call-update) | async-done | bytes 3538960 | tf_op jit(solution)/shard_map/all_gather | solution.py:55
  71.9 0.0 copy-start
  71.9 2.7 %convolution_bitcast_fusion = f32[3,3,16,4,18,128]{5,2,4,3,1,0:T(8,128)S(1)} fusion(bf16[128,6,18,128]{3,0,2,1:T(8,128)(2,1)} %all-gather.2.cloned.1.call-done, bf16[3,3,3,16,128]{4,3,2,1,0:T(8,128)(2,1)} %param.4), kind=kOutput, calls=%fused_computation | convolution fusion | flops 339738624 | bytes 7704576 | tf_op jit(solution)/shard_map/dot_general | solution.py:33
  74.6 0.0 copy-done.1
  74.6 0.1 copy-done
  74.6 0.8 convolution_bitcast_fusion.1
  75.5 0.8 convolution_bitcast_fusion.2
  76.3 0.0 copy-start.2
  76.3 0.3 fusion.2
  76.7 0.3 fusion.8
  77.0 0.2 slice.191
  77.2 0.0 copy-done.2
  77.2 0.4 fusion
  77.6 0.8 copy.21
  (5 shorter events, 0.1 us)
Async XLA Ops:
  6.5 65.4 %all-gather.2.cloned.1.call-start = ((), (), s32[]{:S(2)}) async-start(), calls=%async_computation | async-start | bytes 3981312 | tf_op jit(solution)/shard_map/all_gather | solution.py:55
  7.5 6.2 %collective-permute-start = (bf16[16,1,16,128]{3,0,2,1:T(8,128)(2,1)S(1)}, bf16[16,1,16,128]{3,0,2,1:T(8,128)(2,1)S(1)}, u32[]{:S(2)}, u32[]{:S(2)}) collective-permute-start(bf16[16,1,16,128]{3,0,2,1:T(8,128)(2,1)S(1)} %copy.37), channel_id=1, source_target_pairs={{0,16},{16,32},{32,48},{48,64},{64,80},{80,96},{96,112},{112,128},... | collective-permute-start | bytes 196616 | tf_op jit(solution)/shard_map/ppermute | solution.py:14
  12.3 5.6 %collective-permute-start.1 = (bf16[16,1,16,128]{3,0,2,1:T(8,128)(2,1)S(1)}, bf16[16,1,16,128]{3,0,2,1:T(8,128)(2,1)S(1)}, u32[]{:S(2)}, u32[]{:S(2)}) collective-permute-start(bf16[16,1,16,128]{3,0,2,1:T(8,128)(2,1)S(1)} %copy.38), channel_id=1, source_target_pairs={{16,0},{32,16},{48,32},{64,48},{80,64},{96,80},{112,96},{128,112},... | collective-permute-start | bytes 196616 | tf_op jit(solution)/shard_map/ppermute | solution.py:15
  18.0 4.5 %collective-permute-start.2 = (bf16[16,6,1,128]{3,0,2,1:T(8,128)(2,1)S(1)}, bf16[16,6,1,128]{3,0,2,1:T(8,128)(2,1)S(1)}, u32[]{:S(2)}, u32[]{:S(2)}) collective-permute-start(bf16[16,6,1,128]{3,0,2,1:T(8,128)(2,1)S(1)} %get-tuple-element.5), channel_id=1, source_target_pairs={{0,8},{1,9},{2,10},{3,11},{4,12},{5,13},{6,14},{7,15},{16,24},{17,... | collective-permute-start | bytes 73736 | tf_op jit(solution)/shard_map/ppermute | solution.py:14
  21.2 4.6 %collective-permute-start.3 = (bf16[16,6,1,128]{3,0,2,1:T(8,128)(2,1)S(1)}, bf16[16,6,1,128]{3,0,2,1:T(8,128)(2,1)S(1)}, u32[]{:S(2)}, u32[]{:S(2)}) collective-permute-start(bf16[16,6,1,128]{3,0,2,1:T(8,128)(2,1)S(1)} %get-tuple-element.6), channel_id=1, source_target_pairs={{8,0},{9,1},{10,2},{11,3},{12,4},{13,5},{14,6},{15,7},{24,16},{25,... | collective-permute-start | bytes 73736 | tf_op jit(solution)/shard_map/ppermute | solution.py:15
  26.7 47.9 %copy-start.1 = (bf16[3,3,3,16,128]{4,3,2,1,0:T(8,128)(2,1)S(1)}, bf16[3,3,3,16,128]{4,3,2,1,0:T(8,128)(2,1)}, u32[]{:S(2)}) copy-start(bf16[3,3,3,16,128]{4,3,2,1,0:T(8,128)(2,1)} %param.4) | copy-start | bytes 331780
  71.9 2.7 %copy-start = (bf16[128,6,18,128]{3,0,2,1:T(8,128)(2,1)S(1)}, bf16[128,6,18,128]{3,0,2,1:T(8,128)(2,1)}, u32[]{:S(2)}) copy-start(bf16[128,6,18,128]{3,0,2,1:T(8,128)(2,1)} %all-gather.2.cloned.1.call-done) | copy-start | bytes 10616836
  76.3 0.8 copy-start.2
Sparse Core Ops, SparseCore 0:
  26.8 45.0 all-gather.1
where the time goes:
time: 85.4 us; the launch traced here: 85.2 us
  waiting for transfers between devices  51.7 us (61%)
  between operations  13.5 us (16%)
  starting transfers between devices  10.6 us (12%)
  matrix products  4.34 us (5%)
  local copies, waits for them, and re-layouts  3.13 us (4%)
  other arithmetic  1.86 us (2%)
    all_gather x1, waiting for transfers between devices, per_device(): gathered = lax.all_gather(padded, 'col', axis=0, tiled=True)  45.2 us
    ppermute x2, starting transfers between devices, with_halo(): before = lax.ppermute(last, axis, up)  8.02 us
    ppermute x2, waiting for transfers between devices, with_halo(): after = lax.ppermute(first, axis, down)  6.47 us
    dot_general x3, matrix products, convolve(): lax.dot_general(weights[depth_tap], planes, (((3,), (0,)), ((), ())), pre...  4.34 us
    ppermute x2, starting transfers between devices, with_halo(): after = lax.ppermute(first, axis, down)  2.58 us
  transfers between devices with their start and end apart: 5, of which 3 were waited for; matrix products, arithmetic and copies ran while one was open for 1% of the time, Pallas kernels for 0%

commit v1 on v0

v1 whole, which is shorter than its diff:
```python
import jax
import jax.numpy as jnp
from jax import lax
from jax.experimental import pallas as pl
from jax.experimental.pallas import tpu as pltpu
from jax.sharding import PartitionSpec as P

MESH = pl.DeviceIdType.MESH

ORDER = (0, 1, 6, 2, 3, 4, 5)
PLANE = {0: 1, 1: 2, 2: 3, 3: 4, 4: 0, 5: 5}
RELAY_RIGHT = (0, 2, 4)


def kernel(x_ref, k_ref, b_ref, o_ref, g, wb, acc, local_sem, hs, hr, ls, lr, rs, rr, xs, xr, ps, pr):
    dev, ha, col = lax.axis_index("dev"), lax.axis_index("ha"), lax.axis_index("col")
    devs = lax.axis_size("dev")
    chip, core = col // 2, lax.rem(col, 2)
    right = 2 * lax.rem(chip + 1, 4) + core
    left = 2 * lax.rem(chip + 3, 4) + core
    partner = 2 * chip + 1 - core
    up, down = lax.rem(dev + 1, devs), lax.rem(dev + devs - 1, devs)
    other = 1 - ha

    barrier = pltpu.get_barrier_semaphore()
    for target in (
        (dev, ha, right), (dev, ha, left), (dev, ha, partner), (up, ha, col), (down, ha, col),
        (dev, other, col), (up, other, col), (down, other, col),
    ):
        pl.semaphore_signal(barrier, inc=1, device_id=target, device_id_type=MESH)

    def slot(of_chip):
        return pl.ds(pl.multiple_of(core * 64 + of_chip * 16, 16), 16)

    mine = slot(chip)
    halo_row = 17 * other

    local = pltpu.make_async_copy(x_ref, g.at[1:5, 1:17, mine], local_sem)
    local.start()
    g[:, pl.ds(17 * ha, 1)] = jnp.zeros((6, 1, 128, 128), jnp.bfloat16)
    pl.semaphore_wait(barrier, 8)

    def remote(src, dst, send, recv, target):
        return pltpu.make_async_remote_copy(
            src_ref=src, dst_ref=dst, send_sem=send, recv_sem=recv,
            device_id=target, device_id_type=MESH,
        )

    edge = 15 * other
    halos = [
        remote(x_ref.at[3], g.at[0, 1:17, mine], hs.at[0], hr.at[0], (up, ha, col)),
        remote(x_ref.at[0], g.at[5, 1:17, mine], hs.at[1], hr.at[1], (down, ha, col)),
        remote(x_ref.at[:, edge], g.at[1:5, 17 * ha, mine], hs.at[2], hr.at[2], (dev, other, col)),
        remote(x_ref.at[3, edge], g.at[0, 17 * ha, mine], hs.at[3], hr.at[3], (up, other, col)),
        remote(x_ref.at[0, edge], g.at[5, 17 * ha, mine], hs.at[4], hr.at[4], (down, other, col)),
    ]
    for i in (2, 3, 4, 0, 1):
        halos[i].start()

    def part(unit, channels):
        if unit == 6:
            return g.at[:, halo_row, channels]
        return g.at[PLANE[unit], 1:17, channels]

    sends = []

    def own_source(unit):
        return x_ref.at[unit] if unit < 4 else part(unit, mine)

    def send_own(unit):
        if unit == 4:
            halos[0].wait_recv()
        if unit == 5:
            halos[1].wait_recv()
        if unit == 6:
            for i in (2, 3, 4):
                halos[i].wait_recv()
        for target, send, recv in ((right, ls, lr), (left, rs, rr)):
            copy = remote(own_source(unit), part(unit, mine), send.at[unit], recv.at[unit], (dev, ha, target))
            copy.start()
            sends.append(copy)

    def arrival(unit, channels, send, recv):
        return remote(part(unit, channels), part(unit, channels), send.at[unit], recv.at[unit], (dev, ha, partner))

    from_left = slot(lax.rem(chip + 3, 4))
    from_right = slot(lax.rem(chip + 1, 4))
    across = slot(lax.rem(chip + 2, 4))

    def relay(unit):
        arrival(unit, from_left, ls, lr).wait_recv()
        arrival(unit, from_right, rs, rr).wait_recv()
        channels, target = (from_left, right) if unit in RELAY_RIGHT else (from_right, left)
        copy = remote(part(unit, channels), part(unit, channels), xs.at[unit], xr.at[unit], (dev, ha, target))
        copy.start()
        sends.append(copy)

    my_half = pl.ds(pl.multiple_of(core * 64, 64), 64)
    its_half = pl.ds(pl.multiple_of((1 - core) * 64, 64), 64)

    def forward(unit):
        arrival(unit, across, xs, xr).wait_recv()
        copy = remote(part(unit, my_half), part(unit, my_half), ps.at[unit], pr.at[unit], (dev, ha, partner))
        copy.start()
        sends.append(copy)

    send_own(ORDER[0])
    send_own(ORDER[1])

    row = lax.broadcasted_iota(jnp.int32, (128, 128), 0)
    column = lax.broadcasted_iota(jnp.int32, (128, 128), 1)
    place = (row // 16 % 2) * 64 + (row // 32) * 16 + row % 16
    permutation = jnp.where(place == column, 1.0, 0.0).astype(jnp.bfloat16)
    for a in range(3):
        for b in range(3):
            taps = k_ref[a, b].reshape(48, 128)
            taps = jnp.dot(taps, permutation, preferred_element_type=jnp.float32)
            wb[a * 48 : a * 48 + 48, b * 128 : b * 128 + 128] = taps.astype(jnp.bfloat16)
    eye = lax.broadcasted_iota(jnp.int32, (16, 16), 0) == lax.broadcasted_iota(jnp.int32, (16, 16), 1)
    bias = jnp.sum(jnp.where(eye, b_ref[...], 0.0), axis=1, keepdims=True)

    first = {0: True, 1: True, 2: True, 3: True}

    def compute(plane):
        taps = [a for a in range(3) if 0 <= plane - a < 4]
        low, high = taps[0] * 48, taps[-1] * 48 + 48
        fresh = {a: first[plane - a] for a in taps}
        for a in taps:
            first[plane - a] = False

        def pair(j, carry):
            cells = jnp.concatenate(
                [g[plane, pl.ds(2 * j, 3)].reshape(384, 128), g[plane, pl.ds(2 * j + 1, 3)].reshape(384, 128)],
                axis=1,
            )
            out = jnp.dot(wb[low:high, :], cells, preferred_element_type=jnp.float32)
            for a in taps:
                value = out[a * 48 - low : a * 48 - low + 48]
                if fresh[a]:
                    acc[plane - a, j] = value
                else:
                    acc[plane - a, j] += value
            return carry

        lax.fori_loop(0, 8, pair, 0, unroll=2)

    lane = lax.broadcasted_iota(jnp.int32, (16, 128), 1)

    def finish(d):
        def pair(j, carry):
            for half in range(2):
                lanes = slice(half * 128, half * 128 + 128)
                before = pltpu.roll(acc[d, j, 0:16, lanes], 1, 1)
                after = pltpu.roll(acc[d, j, 32:48, lanes], 127, 1)
                total = acc[d, j, 16:32, lanes] + bias
                total += jnp.where(lane == 0, 0.0, before) + jnp.where(lane == 127, 0.0, after)
                o_ref[d, 2 * j + half] = jnp.where(total >= 0, total, 0.3 * total).astype(jnp.bfloat16)
            return carry

        lax.fori_loop(0, 8, pair, 0, unroll=2)

    waiting = []
    done = []
    steps = len(ORDER)
    for step in range(steps + 2):
        if step < steps:
            relay(ORDER[step])
        if step + 2 < steps:
            send_own(ORDER[step + 2])
        if 1 <= step <= steps:
            if step == 1:
                local.wait()
            forward(ORDER[step - 1])
        if step >= 2:
            unit = ORDER[step - 2]
            arrival(unit, its_half, ps, pr).wait_recv()
            done.append(unit)
            if unit != 6:
                waiting.append(PLANE[unit])
            if 6 in done:
                for plane in waiting:
                    if plane == 0:
                        pl.when(dev > 0)(lambda: compute(0))
                    elif plane == 5:
                        pl.when(dev < devs - 1)(lambda: compute(5))
                    else:
                        compute(plane)
                    if plane == 3:
                        finish(1)
                    if plane == 4:
                        finish(2)
                    if plane == 0:
                        finish(0)
                    if plane == 5:
                        finish(3)
                waiting = []
    for copy in halos + sends:
        copy.wait_send()


def per_device(features, weights, channel_bias):
    rows = jnp.transpose(features, (1, 2, 0, 3))
    dma = pltpu.SemaphoreType.DMA
    out = pl.pallas_call(
        kernel,
        out_shape=jax.ShapeDtypeStruct((4, 16, 16, 128), jnp.bfloat16),
        in_specs=[pl.BlockSpec(memory_space=pltpu.VMEM)] * 3,
        out_specs=pl.BlockSpec(memory_space=pltpu.VMEM),
        scratch_shapes=[
            pltpu.VMEM((6, 18, 128, 128), jnp.bfloat16),
            pltpu.VMEM((144, 384), jnp.bfloat16),
            pltpu.VMEM((4, 8, 48, 256), jnp.float32),
            dma(()),
            dma((5,)), dma((5,)),
            dma((7,)), dma((7,)), dma((7,)), dma((7,)),
            dma((7,)), dma((7,)), dma((7,)), dma((7,)),
        ],
        compiler_params=pltpu.CompilerParams(collective_id=0, has_side_effects=True),
    )(rows, weights, channel_bias[None, :])
    return jnp.transpose(out, (2, 0, 1, 3))


def solution(mesh):
    in_specs = (P("col", "dev", "ha", None), P(None, None, None, "col", None), P("col"))
    out_specs = P("col", "dev", "ha", None)
    return jax.shard_map(
        per_device, mesh=mesh, in_specs=in_specs, out_specs=out_specs, check_vma=False
    )
```

time: 85.4 us -> 44.3 us (0.52)
  the two profiles are of different devices: /device:TPU:1 before, /device:TPU:7 now
where the time goes in v1:
time: 44.3 us; the launch traced here: 44.2 us
  Pallas kernels  40.6 us (92%)
  local copies, waits for them, and re-layouts  3.55 us (8%)
    pallas_call x1, Pallas kernels, per_device(): pl.pallas_call(kernel, out_shape=jax.ShapeDtypeStruct((4, 16, 16, 128), j...  40.6 us
    unnamed x1, local copies, waits for them, and re-layouts  1.82 us
    transpose x1, local copies, waits for them, and re-layouts, per_device(): return jnp.transpose(out, (2, 0, 1, 3))  1.72 us

profile of v1, /device:TPU:7, one launch (start us, length us, event | category | flops | bytes accessed | tf_op | source)
XLA Modules:
  0.0 44.2 jit_solution(15557575035517805945)
XLA Ops:
  0.0 1.8 %copy.7 = bf16[16,4,16,128]{3,0,2,1:T(8,128)(2,1)} copy(bf16[16,4,16,128]{3,2,1,0:T(8,128)(2,1)} %param.3) | data formatting | bytes 524288 | tf_op args[0]
  1.8 40.6 %shard_map.37 = bf16[4,16,16,128]{3,2,1,0:T(8,128)(2,1)} custom-call(bf16[4,16,16,128]{3,2,1,0:T(8,128)(2,1)} %bitcast.6, bf16[3,3,3,16,128]{4,3,2,1,0:T(8,128)(2,1)} %k_ref.1, f32[1,16]{1,0:T(1,128)} %bitcast.7), custom_call_target="tpu_custom_call" | custom-call | tf_op jit(solution)/shard_map/pallas_call | solution.py:204
  42.4 1.7 %copy.5 = bf16[16,4,16,128]{3,2,1,0:T(8,128)(2,1)} copy(bf16[16,4,16,128]{3,0,2,1:T(8,128)(2,1)} %bitcast.5) | data formatting | bytes 524288 | tf_op jit(solution)/shard_map/transpose | solution.py:220

commit v2 on v1

v2 whole, which is shorter than its diff:
```python
import jax
import jax.numpy as jnp
from jax import lax
from jax.experimental import pallas as pl
from jax.experimental.pallas import tpu as pltpu
from jax.sharding import PartitionSpec as P

MESH = pl.DeviceIdType.MESH

ORDER = (0, 3, 1, 2, 6)
TAIL = (4, 5)
PLANE = {0: 1, 1: 2, 2: 3, 3: 4, 4: 0, 5: 5}
RELAY_RIGHT = (0, 1, 6)


def kernel(x_ref, k_hbm, b_hbm, o_hbm, g, wb, acc, k_ref, b_ref, o_ref, local_sem, os, hs, hr, ls, lr, rs, rr, xs, xr, ps, pr, zs, zr):
    dev, ha, col = lax.axis_index("dev"), lax.axis_index("ha"), lax.axis_index("col")
    devs = lax.axis_size("dev")
    chip, core = col // 2, lax.rem(col, 2)
    right = 2 * lax.rem(chip + 1, 4) + core
    left = 2 * lax.rem(chip + 3, 4) + core
    partner = 2 * chip + 1 - core
    up, down = lax.rem(dev + 1, devs), lax.rem(dev + devs - 1, devs)
    other = 1 - ha

    barrier = pltpu.get_barrier_semaphore()
    has_up, has_down = dev < devs - 1, dev > 0

    def greet(*targets):
        for target in targets:
            pl.semaphore_signal(barrier, inc=1, device_id=target, device_id_type=MESH)

    greet((dev, ha, right), (dev, ha, left), (dev, ha, partner), (dev, other, col))
    pl.when(has_up)(lambda: greet((up, ha, col), (up, other, col)))
    pl.when(has_down)(lambda: greet((down, ha, col), (down, other, col)))

    mine = chip
    halo_row = 17 * other

    local = pltpu.make_async_copy(x_ref, g.at[mine, core, 1:5, 1:17], local_sem.at[0])
    local.start()
    parameters = [
        pltpu.make_async_copy(k_hbm, k_ref, local_sem.at[1]),
        pltpu.make_async_copy(b_hbm, b_ref, local_sem.at[2]),
    ]
    for copy in parameters:
        copy.start()
    g[:, :, :, pl.ds(17 * ha, 1)] = jnp.zeros((4, 2, 6, 1, 16, 128), jnp.bfloat16)

    @pl.when(jnp.logical_not(has_down))
    def _():
        g[mine, core, 0, halo_row] = jnp.zeros((16, 128), jnp.bfloat16)

    @pl.when(jnp.logical_not(has_up))
    def _():
        g[mine, core, 5, halo_row] = jnp.zeros((16, 128), jnp.bfloat16)

    pl.semaphore_wait(barrier, 4 + 2 * has_up.astype(jnp.int32) + 2 * has_down.astype(jnp.int32))

    def remote(src, dst, send, recv, target):
        return pltpu.make_async_remote_copy(
            src_ref=src, dst_ref=dst, send_sem=send, recv_sem=recv,
            device_id=target, device_id_type=MESH,
        )

    edge = 15 * other
    halos = [
        remote(x_ref.at[3], g.at[mine, core, 0, 1:17], hs.at[0], hr.at[0], (up, ha, col)),
        remote(x_ref.at[0], g.at[mine, core, 5, 1:17], hs.at[1], hr.at[1], (down, ha, col)),
        remote(x_ref.at[:, edge], g.at[mine, core, 1:5, 17 * ha], hs.at[2], hr.at[2], (dev, other, col)),
        remote(x_ref.at[3, edge], g.at[mine, core, 0, 17 * ha], hs.at[3], hr.at[3], (up, other, col)),
        remote(x_ref.at[0, edge], g.at[mine, core, 5, 17 * ha], hs.at[4], hr.at[4], (down, other, col)),
    ]
    def part(unit, chips, side=core):
        if unit == 6:
            return g.at[chips, side, :, halo_row]
        return g.at[chips, side, PLANE[unit], 1:17]

    to = {0: has_up, 1: has_down, 2: None, 3: has_up, 4: has_down}
    come = {0: has_down, 1: has_up, 2: None, 3: has_down, 4: has_up}
    exists = {4: has_down, 5: has_up}

    def when(condition, act):
        if condition is None:
            act()
        else:
            pl.when(condition)(act)

    sends = []

    def own_source(unit):
        return x_ref.at[unit] if unit < 4 else part(unit, mine)

    def send(unit, target, send_sems, recv_sems):
        copy = remote(own_source(unit), part(unit, mine), send_sems.at[unit], recv_sems.at[unit], (dev, ha, target))
        when(exists.get(unit), copy.start)
        sends.append((exists.get(unit), copy))

    def send_own(unit):
        if unit == 6:
            for i in (2, 3, 4):
                when(come[i], halos[i].wait_recv)
        if unit in (4, 5):
            when(come[unit - 4], halos[unit - 4].wait_recv)
        if unit != 5:
            send(unit, right, ls, lr)
        if unit != 4:
            send(unit, left, rs, rr)

    def arrival(unit, chips, send, recv, side=core):
        return remote(part(unit, chips, side), part(unit, chips, side), send.at[unit], recv.at[unit], (dev, ha, partner))

    from_left = lax.rem(chip + 3, 4)
    from_right = lax.rem(chip + 1, 4)
    across = lax.rem(chip + 2, 4)

    def relay(unit):
        arrival(unit, from_left, ls, lr).wait_recv()
        arrival(unit, from_right, rs, rr).wait_recv()
        chips, target = (from_left, right) if unit in RELAY_RIGHT else (from_right, left)
        copy = remote(part(unit, chips), part(unit, chips), xs.at[unit], xr.at[unit], (dev, ha, target))
        copy.start()
        sends.append((None, copy))
        if unit == 0:
            when(has_down, to_depth[0].start)
        if unit == 3:
            when(has_up, to_depth[2].start)

    def depth(chips, halo, index):
        plane, target = (4, up) if halo == 0 else (1, down)
        return remote(
            g.at[chips, core, plane, 1:17], g.at[chips, core, halo, 1:17], zs.at[index], zr.at[index], (target, ha, col)
        )

    to_depth = [depth(from_left, 5, 0), depth(across, 5, 1), depth(from_right, 0, 2), depth(across, 0, 3)]
    every = pl.ds(0, 4)

    def forward(unit):
        def whole():
            if unit == 4:
                arrival(unit, from_left, ls, lr).wait_recv()
                to_depth[2].wait_recv()
                to_depth[3].wait_recv()
            elif unit == 5:
                arrival(unit, from_right, rs, rr).wait_recv()
                to_depth[0].wait_recv()
                to_depth[1].wait_recv()
            else:
                arrival(unit, across, xs, xr).wait_recv()

        copy = remote(part(unit, every), part(unit, every), ps.at[unit], pr.at[unit], (dev, ha, partner))
        when(exists.get(unit), whole)
        when(exists.get(unit), copy.start)
        sends.append((exists.get(unit), copy))
        if unit == 0:
            when(has_down, to_depth[1].start)
        if unit == 3:
            when(has_up, to_depth[3].start)

    send_own(ORDER[0])
    for i in (0, 1, 2, 3, 4):
        when(to[i], halos[i].start)
    send_own(ORDER[1])

    for copy in parameters:
        copy.wait()
    for a in range(3):
        for b in range(3):
            wb[a * 48 : a * 48 + 48, b * 128 : b * 128 + 128] = k_ref[a, b].reshape(48, 128)
    eye = lax.broadcasted_iota(jnp.int32, (16, 16), 0) == lax.broadcasted_iota(jnp.int32, (16, 16), 1)
    bias = jnp.sum(jnp.where(eye, b_ref[...], 0.0), axis=1, keepdims=True)

    seen = set()

    def compute(plane, pairs):
        taps = [a for a in range(3) if 0 <= plane - a < 4]
        low, high = taps[0] * 48, taps[-1] * 48 + 48
        fresh = {a: (plane - a, pairs) not in seen and pairs != "all" for a in taps}
        seen.update((plane - a, pairs) for a in taps)

        def pair(j, carry):
            rows = [g[:, :, plane, 2 * j + i].reshape(128, 128) for i in range(4)]
            cells = jnp.concatenate([jnp.concatenate(rows[i : i + 2], axis=1) for i in range(3)], axis=0)
            out = jnp.dot(wb[low:high, :], cells, preferred_element_type=jnp.float32)
            for a in taps:
                value = out[a * 48 - low : a * 48 - low + 48]
                if fresh[a]:
                    acc[plane - a, j] = value
                else:
                    acc[plane - a, j] += value
            return carry

        if pairs == "inner":
            lax.fori_loop(0, 7, lambda i, carry: pair(ha + i, carry), 0, unroll=7)
        elif pairs == "edge":
            pair(7 * other, 0)
        else:
            lax.fori_loop(0, 8, pair, 0, unroll=4)

    lane = lax.broadcasted_iota(jnp.int32, (16, 128), 1)

    def finish(d):
        def pair(j, carry):
            for half in range(2):
                lanes = slice(half * 128, half * 128 + 128)
                before = pltpu.roll(acc[d, j, 0:16, lanes], 1, 1)
                after = pltpu.roll(acc[d, j, 32:48, lanes], 127, 1)
                total = acc[d, j, 16:32, lanes] + bias
                total += jnp.where(lane == 0, 0.0, before) + jnp.where(lane == 127, 0.0, after)
                o_ref[d, 2 * j + half] = jnp.where(total >= 0, total, 0.3 * total).astype(jnp.bfloat16)
            return carry

        lax.fori_loop(0, 8, pair, 0, unroll=4)
        results[d].start()

    results = [pltpu.make_async_copy(o_ref.at[d], o_hbm.at[d], os.at[d]) for d in range(4)]
    queue = ORDER + TAIL
    steps = len(queue)
    for step in range(steps + 2):
        if step < len(ORDER):
            relay(queue[step])
        if step + 2 < steps:
            send_own(queue[step + 2])
        if 1 <= step <= steps:
            if step == 1:
                local.wait()
            forward(queue[step - 1])
        if step >= 2:
            unit = queue[step - 2]
            when(exists.get(unit), arrival(unit, every, ps, pr, 1 - core).wait_recv)
            if unit < 4:
                compute(PLANE[unit], "inner")
            elif unit == 6:
                for own in ORDER[:4]:
                    compute(PLANE[own], "edge")
                finish(1)
                finish(2)
            else:
                when(exists[unit], lambda: compute(PLANE[unit], "all"))
                finish(0 if unit == 4 else 3)
    for i in range(5):
        when(to[i], halos[i].wait_send)
    for i in range(4):
        when(has_down if i < 2 else has_up, to_depth[i].wait_send)
    for condition, copy in sends:
        when(condition, copy.wait_send)
    for copy in results:
        copy.wait()


def per_device(features, weights, channel_bias):
    rows = jnp.transpose(features, (1, 2, 0, 3))
    dma = pltpu.SemaphoreType.DMA
    out = pl.pallas_call(
        kernel,
        out_shape=jax.ShapeDtypeStruct((4, 16, 16, 128), jnp.bfloat16),
        in_specs=[pl.BlockSpec(memory_space=pl.ANY)] * 3,
        out_specs=pl.BlockSpec(memory_space=pl.ANY),
        scratch_shapes=[
            pltpu.VMEM((4, 2, 6, 18, 16, 128), jnp.bfloat16),
            pltpu.VMEM((144, 384), jnp.bfloat16),
            pltpu.VMEM((4, 8, 48, 256), jnp.float32),
            pltpu.VMEM((3, 3, 3, 16, 128), jnp.bfloat16),
            pltpu.VMEM((1, 16), jnp.float32),
            pltpu.VMEM((4, 16, 16, 128), jnp.bfloat16),
            dma((3,)), dma((4,)),
            dma((5,)), dma((5,)),
            dma((7,)), dma((7,)), dma((7,)), dma((7,)),
            dma((7,)), dma((7,)), dma((7,)), dma((7,)),
            dma((4,)), dma((4,)),
        ],
        compiler_params=pltpu.CompilerParams(collective_id=0, has_side_effects=True),
    )(rows, weights, channel_bias[None, :])
    return jnp.transpose(out, (2, 0, 1, 3))


def solution(mesh):
    in_specs = (P("col", "dev", "ha", None), P(None, None, None, "col", None), P("col"))
    out_specs = P("col", "dev", "ha", None)
    return jax.shard_map(
        per_device, mesh=mesh, in_specs=in_specs, out_specs=out_specs, check_vma=False
    )
```

time: 44.3 us -> 37.9 us (0.86)
  the two profiles are of different devices: /device:TPU:7 before, /device:TPU:56 now
where the time goes in v2:
time: 37.9 us; the launch traced here: 37.5 us
  Pallas kernels  33.9 us (89%)
  local copies, waits for them, and re-layouts  3.55 us (9%)
    pallas_call x1, Pallas kernels, per_device(): pl.pallas_call(kernel, out_shape=jax.ShapeDtypeStruct((4, 16, 16, 128), j...  33.9 us
    unnamed x1, local copies, waits for them, and re-layouts  1.82 us
    transpose x1, local copies, waits for them, and re-layouts, per_device(): return jnp.transpose(out, (2, 0, 1, 3))  1.72 us

profile of v2, /device:TPU:56, one launch (start us, length us, event | category | flops | bytes accessed | tf_op | source)
XLA Modules:
  0.0 37.5 jit_solution(8619374416898357962)
XLA Ops:
  0.0 1.8 %copy.7 = bf16[16,4,16,128]{3,0,2,1:T(8,128)(2,1)} copy(bf16[16,4,16,128]{3,2,1,0:T(8,128)(2,1)} %param.3) | data formatting | bytes 524288 | tf_op args[0]
  1.8 33.9 %shard_map.37 = bf16[4,16,16,128]{3,2,1,0:T(8,128)(2,1)} custom-call(bf16[4,16,16,128]{3,2,1,0:T(8,128)(2,1)} %bitcast.6, bf16[3,3,3,16,128]{4,3,2,1,0:T(8,128)(2,1)} %k_hbm.1, f32[1,16]{1,0:T(1,128)} %bitcast.7), custom_call_target="tpu_custom_call" | custom-call | tf_op jit(solution)/shard_map/pallas_call | solution.py:254
  35.8 1.7 %copy.5 = bf16[16,4,16,128]{3,2,1,0:T(8,128)(2,1)} copy(bf16[16,4,16,128]{3,0,2,1:T(8,128)(2,1)} %bitcast.5) | data formatting | bytes 524288 | tf_op jit(solution)/shard_map/transpose | solution.py:274

commit v3 on v2

--- a/solution.py
+++ b/solution.py
@@ -7,13 +7,14 @@
 
 MESH = pl.DeviceIdType.MESH
 
-ORDER = (0, 3, 1, 2, 6)
+ORDER = (3, 0, 1, 2, 6)
 TAIL = (4, 5)
+LATE_STEP = 2
 PLANE = {0: 1, 1: 2, 2: 3, 3: 4, 4: 0, 5: 5}
 RELAY_RIGHT = (0, 1, 6)
 
 
-def kernel(x_ref, k_hbm, b_hbm, o_hbm, g, wb, acc, k_ref, b_ref, o_ref, local_sem, os, hs, hr, ls, lr, rs, rr, xs, xr, ps, pr, zs, zr):
+def kernel(x_ref, k_hbm, b_hbm, o_hbm, g, wb, acc, k_ref, b_ref, o_ref, local_sem, os, ready, hs, hr, ls, lr, rs, rr, xs, xr, ps, pr, zs, zr):
     dev, ha, col = lax.axis_index("dev"), lax.axis_index("ha"), lax.axis_index("col")
     devs = lax.axis_size("dev")
     chip, core = col // 2, lax.rem(col, 2)
@@ -25,13 +26,17 @@
 
     barrier = pltpu.get_barrier_semaphore()
     has_up, has_down = dev < devs - 1, dev > 0
+    late = jnp.logical_and(has_down, lax.rem(dev, 8) == 0)
+    early = jnp.logical_and(has_up, lax.rem(dev, 8) == 7)
+    greets_up = jnp.logical_and(has_up, jnp.logical_not(early))
+    prompt = jnp.logical_and(has_down, jnp.logical_not(late))
 
     def greet(*targets):
         for target in targets:
             pl.semaphore_signal(barrier, inc=1, device_id=target, device_id_type=MESH)
 
     greet((dev, ha, right), (dev, ha, left), (dev, ha, partner), (dev, other, col))
-    pl.when(has_up)(lambda: greet((up, ha, col), (up, other, col)))
+    pl.when(greets_up)(lambda: greet((up, ha, col), (up, other, col)))
     pl.when(has_down)(lambda: greet((down, ha, col), (down, other, col)))
 
     mine = chip
@@ -55,7 +60,12 @@
     def _():
         g[mine, core, 5, halo_row] = jnp.zeros((16, 128), jnp.bfloat16)
 
-    pl.semaphore_wait(barrier, 4 + 2 * has_up.astype(jnp.int32) + 2 * has_down.astype(jnp.int32))
+    pl.semaphore_wait(barrier, 4 + 2 * has_up.astype(jnp.int32) + 2 * prompt.astype(jnp.int32))
+
+    @pl.when(early)
+    def _():
+        for target in ((up, ha, col), (up, other, col)):
+            pl.semaphore_signal(ready, inc=1, device_id=target, device_id_type=MESH)
 
     def remote(src, dst, send, recv, target):
         return pltpu.make_async_remote_copy(
@@ -122,7 +132,7 @@
         copy.start()
         sends.append((None, copy))
         if unit == 0:
-            when(has_down, to_depth[0].start)
+            when(prompt, to_depth[0].start)
         if unit == 3:
             when(has_up, to_depth[2].start)
 
@@ -153,13 +163,13 @@
         when(exists.get(unit), copy.start)
         sends.append((exists.get(unit), copy))
         if unit == 0:
-            when(has_down, to_depth[1].start)
+            when(prompt, to_depth[1].start)
         if unit == 3:
             when(has_up, to_depth[3].start)
 
     send_own(ORDER[0])
     for i in (0, 1, 2, 3, 4):
-        when(to[i], halos[i].start)
+        when(prompt if i in (1, 4) else to[i], halos[i].start)
     send_own(ORDER[1])
 
     for copy in parameters:
@@ -225,6 +235,14 @@
             if step == 1:
                 local.wait()
             forward(queue[step - 1])
+        if step == LATE_STEP:
+
+            @pl.when(late)
+            def _():
+                pl.semaphore_wait(ready, 2)
+                for copy in (halos[4], halos[1], to_depth[0], to_depth[1]):
+                    copy.start()
+
         if step >= 2:
             unit = queue[step - 2]
             when(exists.get(unit), arrival(unit, every, ps, pr, 1 - core).wait_recv)
@@ -263,7 +281,7 @@
             pltpu.VMEM((3, 3, 3, 16, 128), jnp.bfloat16),
             pltpu.VMEM((1, 16), jnp.float32),
             pltpu.VMEM((4, 16, 16, 128), jnp.bfloat16),
-            dma((3,)), dma((4,)),
+            dma((3,)), dma((4,)), pltpu.SemaphoreType.REGULAR,
             dma((5,)), dma((5,)),
             dma((7,)), dma((7,)), dma((7,)), dma((7,)),
             dma((7,)), dma((7,)), dma((7,)), dma((7,)),

time: 37.9 us -> 36.3 us (0.958)
  Pallas kernels: 33.9 us -> 32.6 us
    pallas_call x1, Pallas kernels: 33.9 us -> 32.6 us  [per_device(): pl.pallas_call(kernel, out_shape=jax.ShapeDtypeStruct((4, 16, 16, 128), j...]
where the time goes in v3:
time: 36.3 us; the launch traced here: 36.1 us
  Pallas kernels  32.6 us (90%)
  local copies, waits for them, and re-layouts  3.55 us (10%)
    pallas_call x1, Pallas kernels, per_device(): pl.pallas_call(kernel, out_shape=jax.ShapeDtypeStruct((4, 16, 16, 128), j...  32.6 us
    unnamed x1, local copies, waits for them, and re-layouts  1.82 us
    transpose x1, local copies, waits for them, and re-layouts, per_device(): return jnp.transpose(out, (2, 0, 1, 3))  1.72 us

profile of v3, /device:TPU:56, one launch (start us, length us, event | category | flops | bytes accessed | tf_op | source)
XLA Modules:
  0.0 36.1 jit_solution(14768715244044141395)
XLA Ops:
  0.0 1.8 %copy.7 = bf16[16,4,16,128]{3,0,2,1:T(8,128)(2,1)} copy(bf16[16,4,16,128]{3,2,1,0:T(8,128)(2,1)} %param.3) | data formatting | bytes 524288 | tf_op args[0]
  1.8 32.6 %shard_map.37 = bf16[4,16,16,128]{3,2,1,0:T(8,128)(2,1)} custom-call(bf16[4,16,16,128]{3,2,1,0:T(8,128)(2,1)} %bitcast.6, bf16[3,3,3,16,128]{4,3,2,1,0:T(8,128)(2,1)} %k_hbm.1, f32[1,16]{1,0:T(1,128)} %bitcast.7), custom_call_target="tpu_custom_call" | custom-call | tf_op jit(solution)/shard_map/pallas_call | solution.py:272
  34.4 1.7 %copy.5 = bf16[16,4,16,128]{3,2,1,0:T(8,128)(2,1)} copy(bf16[16,4,16,128]{3,0,2,1:T(8,128)(2,1)} %bitcast.5) | data formatting | bytes 524288 | tf_op jit(solution)/shard_map/transpose | solution.py:292

commit v4 on v3

--- a/solution.py
+++ b/solution.py
@@ -14,7 +14,7 @@
 RELAY_RIGHT = (0, 1, 6)
 
 
-def kernel(x_ref, k_hbm, b_hbm, o_hbm, g, wb, acc, k_ref, b_ref, o_ref, local_sem, os, ready, hs, hr, ls, lr, rs, rr, xs, xr, ps, pr, zs, zr):
+def kernel(x_hbm, k_hbm, b_hbm, o_hbm, g, wb, acc, k_ref, b_ref, o_ref, x_in, x_ref, local_sem, os, ins, ready, hs, hr, ls, lr, rs, rr, xs, xr, ps, pr, zs, zr):
     dev, ha, col = lax.axis_index("dev"), lax.axis_index("ha"), lax.axis_index("col")
     devs = lax.axis_size("dev")
     chip, core = col // 2, lax.rem(col, 2)
@@ -42,8 +42,10 @@
     mine = chip
     halo_row = 17 * other
 
+    fetch = [pltpu.make_async_copy(x_hbm.at[:, d], x_in.at[:, d], ins.at[d]) for d in range(4)]
+    for d in (3, 0, 1, 2):
+        fetch[d].start()
     local = pltpu.make_async_copy(x_ref, g.at[mine, core, 1:5, 1:17], local_sem.at[0])
-    local.start()
     parameters = [
         pltpu.make_async_copy(k_hbm, k_ref, local_sem.at[1]),
         pltpu.make_async_copy(b_hbm, b_ref, local_sem.at[2]),
@@ -60,6 +62,12 @@
     def _():
         g[mine, core, 5, halo_row] = jnp.zeros((16, 128), jnp.bfloat16)
 
+    for d in (3, 0, 1, 2):
+        fetch[d].wait()
+        for half in range(2):
+            rows = slice(half * 8, half * 8 + 8)
+            x_ref[d, rows] = jnp.swapaxes(x_in[:, d, rows], 0, 1)
+    local.start()
     pl.semaphore_wait(barrier, 4 + 2 * has_up.astype(jnp.int32) + 2 * prompt.astype(jnp.int32))
 
     @pl.when(early)
@@ -267,7 +275,6 @@
 
 
 def per_device(features, weights, channel_bias):
-    rows = jnp.transpose(features, (1, 2, 0, 3))
     dma = pltpu.SemaphoreType.DMA
     out = pl.pallas_call(
         kernel,
@@ -281,14 +288,16 @@
             pltpu.VMEM((3, 3, 3, 16, 128), jnp.bfloat16),
             pltpu.VMEM((1, 16), jnp.float32),
             pltpu.VMEM((4, 16, 16, 128), jnp.bfloat16),
-            dma((3,)), dma((4,)), pltpu.SemaphoreType.REGULAR,
+            pltpu.VMEM((16, 4, 16, 128), jnp.bfloat16),
+            pltpu.VMEM((4, 16, 16, 128), jnp.bfloat16),
+            dma((3,)), dma((4,)), dma((4,)), pltpu.SemaphoreType.REGULAR,
             dma((5,)), dma((5,)),
             dma((7,)), dma((7,)), dma((7,)), dma((7,)),
             dma((7,)), dma((7,)), dma((7,)), dma((7,)),
             dma((4,)), dma((4,)),
         ],
         compiler_params=pltpu.CompilerParams(collective_id=0, has_side_effects=True),
-    )(rows, weights, channel_bias[None, :])
+    )(features, weights, channel_bias[None, :])
     return jnp.transpose(out, (2, 0, 1, 3))
 
 

time: 36.3 us -> 34 us (0.937)
  local copies, waits for them, and re-layouts: 3.55 us -> 1.72 us
  Pallas kernels: 32.6 us -> 32.1 us
    unnamed x1 -> x0, local copies, waits for them, and re-layouts: 1.82 us -> none
    pallas_call x1, Pallas kernels: 32.6 us -> 32.1 us  [per_device(): pl.pallas_call(kernel, out_shape=jax.ShapeDtypeStruct((4, 16, 16, 128), j...]
where the time goes in v4:
time: 34 us; the launch traced here: 33.9 us
  Pallas kernels  32.1 us (94%)
  local copies, waits for them, and re-layouts  1.72 us (5%)
    pallas_call x1, Pallas kernels, per_device(): pl.pallas_call(kernel, out_shape=jax.ShapeDtypeStruct((4, 16, 16, 128), j...  32.1 us
    transpose x1, local copies, waits for them, and re-layouts, per_device(): return jnp.transpose(out, (2, 0, 1, 3))  1.72 us

profile of v4, /device:TPU:56, one launch (start us, length us, event | category | flops | bytes accessed | tf_op | source)
XLA Modules:
  0.0 33.9 jit_solution(6564343768880440193)
XLA Ops:
  0.0 32.1 %shard_map.37 = bf16[4,16,16,128]{3,2,1,0:T(8,128)(2,1)} custom-call(bf16[16,4,16,128]{3,2,1,0:T(8,128)(2,1)} %x_hbm.1, bf16[3,3,3,16,128]{4,3,2,1,0:T(8,128)(2,1)} %k_hbm.1, f32[1,16]{1,0:T(1,128)} %bitcast.3), custom_call_target="tpu_custom_call" | custom-call | tf_op jit(solution)/shard_map/pallas_call | solution.py:279
  32.1 1.7 %copy.4 = bf16[16,4,16,128]{3,2,1,0:T(8,128)(2,1)} copy(bf16[16,4,16,128]{3,0,2,1:T(8,128)(2,1)} %bitcast.2) | data formatting | bytes 524288 | tf_op jit(solution)/shard_map/transpose | solution.py:301

commit v5 on v4

--- a/solution.py
+++ b/solution.py
@@ -14,7 +14,7 @@
 RELAY_RIGHT = (0, 1, 6)
 
 
-def kernel(x_hbm, k_hbm, b_hbm, o_hbm, g, wb, acc, k_ref, b_ref, o_ref, x_in, x_ref, local_sem, os, ins, ready, hs, hr, ls, lr, rs, rr, xs, xr, ps, pr, zs, zr):
+def kernel(x_hbm, k_hbm, b_hbm, o_hbm, g, wb, acc, k_ref, b_ref, o_ref, y_ref, x_in, x_ref, local_sem, os, ins, ready, hs, hr, ls, lr, rs, rr, xs, xr, ps, pr, zs, zr):
     dev, ha, col = lax.axis_index("dev"), lax.axis_index("ha"), lax.axis_index("col")
     devs = lax.axis_size("dev")
     chip, core = col // 2, lax.rem(col, 2)
@@ -229,9 +229,10 @@
             return carry
 
         lax.fori_loop(0, 8, pair, 0, unroll=4)
+        y_ref[:, d] = jnp.swapaxes(o_ref[d], 0, 1)
         results[d].start()
 
-    results = [pltpu.make_async_copy(o_ref.at[d], o_hbm.at[d], os.at[d]) for d in range(4)]
+    results = [pltpu.make_async_copy(y_ref.at[:, d], o_hbm.at[:, d], os.at[d]) for d in range(4)]
     queue = ORDER + TAIL
     steps = len(queue)
     for step in range(steps + 2):
@@ -278,9 +279,9 @@
     dma = pltpu.SemaphoreType.DMA
     out = pl.pallas_call(
         kernel,
-        out_shape=jax.ShapeDtypeStruct((4, 16, 16, 128), jnp.bfloat16),
+        out_shape=pltpu.VMEM((16, 4, 16, 128), jnp.bfloat16),
         in_specs=[pl.BlockSpec(memory_space=pl.ANY)] * 3,
-        out_specs=pl.BlockSpec(memory_space=pl.ANY),
+        out_specs=pl.BlockSpec(memory_space=pltpu.VMEM),
         scratch_shapes=[
             pltpu.VMEM((4, 2, 6, 18, 16, 128), jnp.bfloat16),
             pltpu.VMEM((144, 384), jnp.bfloat16),
@@ -288,6 +289,7 @@
             pltpu.VMEM((3, 3, 3, 16, 128), jnp.bfloat16),
             pltpu.VMEM((1, 16), jnp.float32),
             pltpu.VMEM((4, 16, 16, 128), jnp.bfloat16),
+            pltpu.VMEM((16, 4, 16, 128), jnp.bfloat16),
             pltpu.VMEM((16, 4, 16, 128), jnp.bfloat16),
             pltpu.VMEM((4, 16, 16, 128), jnp.bfloat16),
             dma((3,)), dma((4,)), dma((4,)), pltpu.SemaphoreType.REGULAR,
@@ -298,7 +300,7 @@
         ],
         compiler_params=pltpu.CompilerParams(collective_id=0, has_side_effects=True),
     )(features, weights, channel_bias[None, :])
-    return jnp.transpose(out, (2, 0, 1, 3))
+    return out
 
 
 def solution(mesh):

time: 34 us -> 32.5 us (0.956)
  local copies, waits for them, and re-layouts: 1.72 us -> 0.71 us
  Pallas kernels: 32.1 us -> 31.7 us
    transpose x1 -> x0, local copies, waits for them, and re-layouts: 1.72 us -> none  [per_device(): return jnp.transpose(out, (2, 0, 1, 3))]
    unnamed x0 -> x1, local copies, waits for them, and re-layouts: none -> 0.71 us
    pallas_call x1, Pallas kernels: 32.1 us -> 31.7 us  [per_device(): pl.pallas_call(kernel, out_shape=pltpu.VMEM((16, 4, 16, 128), jnp.bfloat1...]
where the time goes in v5:
time: 32.5 us; the launch traced here: 32.4 us
  Pallas kernels  31.7 us (98%)
  local copies, waits for them, and re-layouts  0.71 us (2%)
    pallas_call x1, Pallas kernels, per_device(): pl.pallas_call(kernel, out_shape=pltpu.VMEM((16, 4, 16, 128), jnp.bfloat1...  31.7 us
    unnamed x1, local copies, waits for them, and re-layouts  0.71 us

profile of v5, /device:TPU:56, one launch (start us, length us, event | category | flops | bytes accessed | tf_op | source)
XLA Modules:
  0.0 32.4 jit_solution(2648408545858321320)
XLA Ops:
  0.0 31.7 %shard_map.37 = bf16[16,4,16,128]{3,2,1,0:T(8,128)(2,1)S(1)} custom-call(bf16[16,4,16,128]{3,2,1,0:T(8,128)(2,1)} %x_hbm.1, bf16[3,3,3,16,128]{4,3,2,1,0:T(8,128)(2,1)} %k_hbm.1, f32[1,16]{1,0:T(1,128)} %bitcast.1), custom_call_target="tpu_custom_call" | custom-call | tf_op jit(solution)/shard_map/pallas_call | solution.py:280
  31.7 0.7 %copy.5 = bf16[16,4,16,128]{3,2,1,0:T(8,128)(2,1)} copy(bf16[16,4,16,128]{3,2,1,0:T(8,128)(2,1)S(1)} %shard_map.37) | data formatting | bytes 524288

commit v6 on v5

--- a/solution.py
+++ b/solution.py
@@ -14,7 +14,7 @@
 RELAY_RIGHT = (0, 1, 6)
 
 
-def kernel(x_hbm, k_hbm, b_hbm, o_hbm, g, wb, acc, k_ref, b_ref, o_ref, y_ref, x_in, x_ref, local_sem, os, ins, ready, hs, hr, ls, lr, rs, rr, xs, xr, ps, pr, zs, zr):
+def kernel(x_hbm, k_hbm, b_hbm, y_ref, g, wb, acc, k_ref, b_ref, o_ref, x_in, x_ref, local_sem, ins, ready, hs, hr, ls, lr, rs, rr, xs, xr, ps, pr, zs, zr):
     dev, ha, col = lax.axis_index("dev"), lax.axis_index("ha"), lax.axis_index("col")
     devs = lax.axis_size("dev")
     chip, core = col // 2, lax.rem(col, 2)
@@ -230,9 +230,7 @@
 
         lax.fori_loop(0, 8, pair, 0, unroll=4)
         y_ref[:, d] = jnp.swapaxes(o_ref[d], 0, 1)
-        results[d].start()
-
-    results = [pltpu.make_async_copy(y_ref.at[:, d], o_hbm.at[:, d], os.at[d]) for d in range(4)]
+
     queue = ORDER + TAIL
     steps = len(queue)
     for step in range(steps + 2):
@@ -271,8 +269,6 @@
         when(has_down if i < 2 else has_up, to_depth[i].wait_send)
     for condition, copy in sends:
         when(condition, copy.wait_send)
-    for copy in results:
-        copy.wait()
 
 
 def per_device(features, weights, channel_bias):
@@ -290,9 +286,8 @@
             pltpu.VMEM((1, 16), jnp.float32),
             pltpu.VMEM((4, 16, 16, 128), jnp.bfloat16),
             pltpu.VMEM((16, 4, 16, 128), jnp.bfloat16),
-            pltpu.VMEM((16, 4, 16, 128), jnp.bfloat16),
             pltpu.VMEM((4, 16, 16, 128), jnp.bfloat16),
-            dma((3,)), dma((4,)), dma((4,)), pltpu.SemaphoreType.REGULAR,
+            dma((3,)), dma((4,)), pltpu.SemaphoreType.REGULAR,
             dma((5,)), dma((5,)),
             dma((7,)), dma((7,)), dma((7,)), dma((7,)),
             dma((7,)), dma((7,)), dma((7,)), dma((7,)),

time: 32.5 us -> 32.5 us (level)
  no operation moved by 1% of the time
where the time goes in v6:
time: 32.5 us; the launch traced here: 32.3 us
  Pallas kernels  31.6 us (97%)
  local copies, waits for them, and re-layouts  0.71 us (2%)
    pallas_call x1, Pallas kernels, per_device(): pl.pallas_call(kernel, out_shape=pltpu.VMEM((16, 4, 16, 128), jnp.bfloat1...  31.6 us
    unnamed x1, local copies, waits for them, and re-layouts  0.71 us

profile of v6, /device:TPU:56, one launch (start us, length us, event | category | flops | bytes accessed | tf_op | source)
XLA Modules:
  0.0 32.3 jit_solution(18413924214169175922)
XLA Ops:
  0.0 31.6 %shard_map.37 = bf16[16,4,16,128]{3,2,1,0:T(8,128)(2,1)S(1)} custom-call(bf16[16,4,16,128]{3,2,1,0:T(8,128)(2,1)} %x_hbm.1, bf16[3,3,3,16,128]{4,3,2,1,0:T(8,128)(2,1)} %k_hbm.1, f32[1,16]{1,0:T(1,128)} %bitcast.1), custom_call_target="tpu_custom_call" | custom-call | tf_op jit(solution)/shard_map/pallas_call | solution.py:276
  31.6 0.7 %copy.5 = bf16[16,4,16,128]{3,2,1,0:T(8,128)(2,1)} copy(bf16[16,4,16,128]{3,2,1,0:T(8,128)(2,1)S(1)} %shard_map.37) | data formatting | bytes 524288
